TPU v7x, 32 devices: a whole 2x2x4 slice. The times are simulated.
32 devices in a mesh: subtree: 4 (over y, core), tile: 8 (over z, x).
Axes of the slice: x: 2, y: 2, z: 4, core: 2. Of those that a mesh axis runs over, the one named last changes fastest.
Arguments:
- interface_stiffness: float32 [4, 4096, 4096], P('subtree', 'tile'), may hold values from -3 to 3
- lower_factor: bfloat16 [4, 4096, 512], P('subtree', 'tile'), may hold values from -0.25 to 0.25
- upper_factor: bfloat16 [4, 512, 4096], P('subtree', None, 'tile'), may hold values from -6 to 6
- modes: bfloat16 [4096, 256], P('tile'), may hold values from -0.09375 to 0.09375
- gyro_rows: int32 [512], replicated, may hold values from 0 to 4095, as said below
- gyro_coupling: float32 [512, 512], replicated, may hold values from -24 to 24
- spin_softening: float32 [512], replicated, may hold values from 0.5 to 8
- speed_index: int32 [2], replicated, may hold values from 0 to 63
Outputs:
- schur: float32 [4096, 4096], P('tile', 'subtree')
- campbell: float32 [2, 256, 256], P(None, 'tile', 'subtree')
Inputs may be any that keep to these rules, and one draw needn't show every extreme that they name: `gyro_rows`: distinct interface degrees of freedom, in whole aligned blocks of 8 consecutive ones.
All inputs are finite; a program needn't handle non-finite values.
Results may differ from a plain program's by a relative error of at most 0.0003.
Values may be sent and summed in bfloat16 or wider, within the bound.
No kernel may reach another device: no remote copies, remote signals or barrier semaphores. Data moves between devices by JAX's collectives and lax.ppermute only.
A program may use at most 64 MiB of HBM per device.

v0:
```python
import jax
import jax.numpy as jnp
from jax import lax
from jax.sharding import PartitionSpec as P

SPEED_STEPS = 64
OMEGA_TOP = 2.0


def partner(block, axis, distance):
    count = lax.axis_size(axis)
    route = []
    for low in range(count):
        high = low | 1 << distance
        if high != low and high < count:
            route += [(low, high), (high, low)]
    return lax.ppermute(block, axis, route)


def shards(
    interface_stiffness,
    lower_factor,
    upper_factor,
    modes,
    gyro_rows,
    gyro_coupling,
    spin_softening,
    speed_index,
):
    tile_count = lax.axis_size("tile")
    branch_count = lax.axis_size("subtree")
    tile_pos = lax.axis_index("tile")
    branch_pos = lax.axis_index("subtree")
    mode_count = modes.shape[1]
    mode_cols = mode_count // branch_count
    mode_rows_dev = mode_count // tile_count
    coupled = jnp.einsum(
        "lrk,lkn->rn",
        lower_factor,
        lax.all_gather(upper_factor, "tile", axis=2, tiled=True),
        preferred_element_type=jnp.float32,
    )
    schur_rows = jnp.sum(interface_stiffness, axis=0) - coupled
    full_width = schur_rows.shape[1]
    own_width = full_width // branch_count
    own_first = branch_pos * own_width
    schur_part = schur_rows
    for level_bit in range(branch_count.bit_length() - 1):
        schur_part = schur_part + partner(schur_part, "subtree", level_bit)
    schur_out = lax.dynamic_slice_in_dim(schur_part, own_first, own_width, 1)
    col_first = branch_pos * mode_cols
    segment = lax.all_gather(modes, "tile", axis=0, tiled=True)
    row_count = segment.shape[0]
    wanted = lax.dynamic_slice_in_dim(segment, col_first, mode_cols, 1).astype(jnp.float32)
    response = jnp.dot(
        schur_part, wanted, precision=lax.Precision.HIGHEST, preferred_element_type=jnp.float32
    )
    inside = (gyro_rows >= 0) & (gyro_rows < row_count)
    taken = jnp.take(segment, jnp.clip(gyro_rows, 0, row_count - 1), axis=0).astype(jnp.float32)
    picked = jnp.where(inside[:, None], taken, jnp.float32(0.0))
    response, picked = (response, picked)
    local_modes = modes.astype(jnp.float32)
    partial_value = jnp.einsum(
        "rm,rc->mc",
        local_modes,
        response,
        precision=lax.Precision.HIGHEST,
        preferred_element_type=jnp.float32,
    )
    stiff_block = lax.psum_scatter(partial_value, "tile", scatter_dimension=0, tiled=True)
    skew_part = 0.5 * (gyro_coupling - gyro_coupling.T)
    left_modes = lax.dynamic_slice_in_dim(picked, tile_pos * mode_rows_dev, mode_rows_dev, 1)
    right_modes = lax.dynamic_slice_in_dim(picked, branch_pos * mode_cols, mode_cols, 1)
    turned = jnp.dot(
        skew_part, right_modes, precision=lax.Precision.HIGHEST, preferred_element_type=jnp.float32
    )
    gyro_block = jnp.einsum(
        "gm,gc->mc",
        left_modes,
        turned,
        precision=lax.Precision.HIGHEST,
        preferred_element_type=jnp.float32,
    )
    spin_block = jnp.einsum(
        "gm,gc->mc",
        left_modes,
        spin_softening[:, None] * right_modes,
        precision=lax.Precision.HIGHEST,
        preferred_element_type=jnp.float32,
    )
    speeds_omega = OMEGA_TOP * (speed_index.astype(jnp.float32) + 1.0) / SPEED_STEPS
    campbell = (
        stiff_block[None]
        + speeds_omega[:, None, None] * gyro_block[None]
        - (speeds_omega * speeds_omega)[:, None, None] * spin_block[None]
    )
    return (schur_out, campbell)


def solution(mesh):
    placed = (
        P("subtree", "tile", None),
        P("subtree", "tile", None),
        P("subtree", None, "tile"),
        P("tile", None),
        P(),
        P(),
        P(),
        P(),
    )
    return jax.shard_map(
        shards,
        mesh=mesh,
        in_specs=placed,
        out_specs=(P("tile", "subtree"), P(None, "tile", "subtree")),
        check_vma=False,
    )
```

profile of v0, /device:TPU:0, one launch (start us, length us, event | category | flops | bytes accessed | tf_op | source)
XLA Modules:
  0.0 391.6 jit_solution(2700897672948704366)
XLA Ops:
  7.2 0.7 all-gather.3.cloned.1.call-update
  8.0 79.8 %all-gather.3.cloned.1.call-done = bf16[1,512,4096]{2,1,0:T(8,128)(2,1)} async-done(((bf16[1,512,512]{2,1,0:T(8,128)(2,1)}), bf16[1,512,4096]{2,1,0:T(8,128)(2,1)}) %all-gather.3.cloned.1.call-update) | async-done | bytes 4194320 | tf_op jit(solution)/shard_map/all_gather | solution.py:40
  87.8 7.0 %bitcast_subtract_fusion = f32[512,4096]{1,0:T(8,128)S(1)} fusion(f32[1,512,4096]{2,1,0:T(8,128)} %param.8, bf16[1,512,4096]{2,1,0:T(8,128)(2,1)} %all-gather.3.cloned.1.call-done, bf16[1,512,512]{2,1,0:T(8,128)(2,1)S(1)} %copy-done), kind=kOutput, calls=%fused_computation.1 | convolution fusion | flops 2149580800 | bytes 21495808 | tf_op jit(solution)/shard_map/lrk,lkn->rn/dot_general | solution.py:37
  94.8 3.2 copy-done.1
  98.1 0.1 collective-permute-start
  98.2 13.3 %collective-permute-done = f32[512,4096]{1,0:T(8,128)} collective-permute-done((f32[512,4096]{1,0:T(8,128)S(1)}, f32[512,4096]{1,0:T(8,128)}, u32[]{:S(2)}, u32[]{:S(2)}) %collective-permute-start) | collective-permute-done | bytes 8388640 | tf_op jit(solution)/shard_map/ppermute | solution.py:17
  111.4 11.1 %add.35 = f32[512,4096]{1,0:T(8,128)} add(f32[512,4096]{1,0:T(8,128)} %copy-done.1, f32[512,4096]{1,0:T(8,128)} %collective-permute-done) | non-fusion elementwise | flops 2097152 | bytes 25165824 | tf_op jit(solution)/shard_map/add | solution.py:49
  122.6 1.5 collective-permute-start.1
  124.1 0.0 reduce-scatter.4.cloned.1.call-start
  124.2 0.3 copy.13
  124.6 46.2 %all-gather.5.cloned.1.call-done = bf16[4096,256]{1,0:T(8,128)(2,1)} async-done(((bf16[512,256]{1,0:T(8,128)(2,1)}), bf16[4096,256]{1,0:T(8,128)(2,1)}) %all-gather.5.cloned.1.call-update) | async-done | bytes 2097168 | tf_op jit(solution)/shard_map/all_gather | solution.py:52
  170.8 3.4 gather_fusion
  174.2 0.2 convert_select_fusion
  174.4 0.8 fusion.8
  175.3 1.1 fusion.2
  176.4 0.7 fusion.13
  177.0 128.3 %collective-permute-done.1 = f32[512,4096]{1,0:T(8,128)} collective-permute-done((f32[512,4096]{1,0:T(8,128)}, f32[512,4096]{1,0:T(8,128)}, u32[]{:S(2)}, u32[]{:S(2)}) %collective-permute-start.1) | collective-permute-done | bytes 8388640 | tf_op jit(solution)/shard_map/ppermute | solution.py:17
  305.4 11.1 %add.36 = f32[512,4096]{1,0:T(8,128)} add(f32[512,4096]{1,0:T(8,128)} %add.35, f32[512,4096]{1,0:T(8,128)} %collective-permute-done.1) | non-fusion elementwise | flops 2097152 | bytes 25165824 | tf_op jit(solution)/shard_map/add | solution.py:49
  316.5 6.7 %fusion.4 = f32[512,64]{1,0:T(8,128)S(1)} fusion(f32[512,4096]{1,0:T(8,128)} %add.36, bf16[4096,256]{1,0:T(8,128)(2,1)S(1)} %copy-done.2, s32[]{:T(128)S(6)} %select_n.24), kind=kOutput, calls=%fused_computation.7 | convolution fusion | flops 1610612736 | bytes 9568260 | tf_op jit(solution)/shard_map/dot_general | solution.py:55
  323.3 0.4 convolution_bitcast_fusion
  323.6 0.8 copy.14
  324.4 3.2 constant_dynamic-slice_fusion
  327.6 56.0 %reduce-scatter.4.cloned.1.call-done = f32[32,64]{1,0:T(8,128)} async-done(((f32[256,64]{1,0:T(8,128)}), f32[32,64]{1,0:T(8,128)}) %reduce-scatter.4.cloned.1.call-update) | async-done | bytes 8208 | tf_op jit(solution)/shard_map/reduce_scatter | solution.py:70
  383.6 1.4 multiply_subtract_fusion
  (23 shorter events, 0.2 us)
Async XLA Ops:
  7.2 80.6 %copy-start = (bf16[1,512,512]{2,1,0:T(8,128)(2,1)S(1)}, bf16[1,512,512]{2,1,0:T(8,128)(2,1)}, u32[]{:S(2)}) copy-start(bf16[1,512,512]{2,1,0:T(8,128)(2,1)} %param.9) | copy-start | bytes 1572868
  7.2 80.6 %all-gather.3.cloned.1.call-start = ((), (), s32[]{:S(2)}) async-start(), calls=%async_computation.1 | async-start | bytes 4718592 | tf_op jit(solution)/shard_map/all_gather | solution.py:40
  7.9 162.9 %all-gather.5.cloned.1.call-start = ((), (), s32[]{:S(2)}) async-start(), calls=%async_computation.2 | async-start | bytes 2359296 | tf_op jit(solution)/shard_map/all_gather | solution.py:52
  94.8 3.2 copy-start.1
  98.1 26.1 %copy-start.3 = (f32[512,512]{1,0:T(8,128)S(1)}, f32[512,512]{1,0:T(8,128)}, u32[]{:S(2)}) copy-start(f32[512,512]{1,0:T(8,128)} %param.13) | copy-start | bytes 3145732
  98.1 26.4 %copy-start.5 = (s32[512]{0:T(512)S(1)}, s32[512]{0:T(512)}, u32[]{:S(2)}) copy-start(s32[512]{0:T(512)} %param.12) | copy-start | bytes 6148
  98.1 26.5 %copy-start.7 = (s32[2]{0:T(128)S(1)}, s32[2]{0:T(128)}, u32[]{:S(2)}) copy-start(s32[2]{0:T(128)} %param.15) | copy-start | bytes 28
  98.1 76.4 %copy-start.6 = (f32[512]{0:T(512)S(1)}, f32[512]{0:T(512)}, u32[]{:S(2)}) copy-start(f32[512]{0:T(512)} %param.14) | copy-start | bytes 6148
  98.1 13.4 %collective-permute-start = (f32[512,4096]{1,0:T(8,128)S(1)}, f32[512,4096]{1,0:T(8,128)}, u32[]{:S(2)}, u32[]{:S(2)}) collective-permute-start(f32[512,4096]{1,0:T(8,128)S(1)} %bitcast_subtract_fusion), channel_id=1, source_target_pairs={{0,8},{8,0},{16,24},{24,16},{1,9},{9,1},{17,25},{25,17},{2,10},{10... | collective-permute-start | bytes 25165832 | tf_op jit(solution)/shard_map/ppermute | solution.py:17
  122.6 182.8 %collective-permute-start.1 = (f32[512,4096]{1,0:T(8,128)}, f32[512,4096]{1,0:T(8,128)}, u32[]{:S(2)}, u32[]{:S(2)}) collective-permute-start(f32[512,4096]{1,0:T(8,128)} %add.35), channel_id=1, source_target_pairs={{0,16},{16,0},{8,24},{24,8},{1,17},{17,1},{9,25},{25,9},{2,18},{18... | collective-permute-start | bytes 25165832 | tf_op jit(solution)/shard_map/ppermute | solution.py:17
  124.1 259.5 %reduce-scatter.4.cloned.1.call-start = ((), (), s32[]{:S(2)}) async-start(), calls=%async_computation.3 | async-start | bytes 147456 | tf_op jit(solution)/shard_map/reduce_scatter | solution.py:70
  177.0 139.5 %copy-start.2 = (bf16[4096,256]{1,0:T(8,128)(2,1)S(1)}, bf16[4096,256]{1,0:T(8,128)(2,1)}, u32[]{:S(2)}) copy-start(bf16[4096,256]{1,0:T(8,128)(2,1)} %all-gather.5.cloned.1.call-done) | copy-start | bytes 6291460
  316.5 6.7 %copy-start.4 = (bf16[512,256]{1,0:T(8,128)(2,1)S(1)}, bf16[512,256]{1,0:T(8,128)(2,1)}, u32[]{:S(2)}) copy-start(bf16[512,256]{1,0:T(8,128)(2,1)} %param.11) | copy-start | bytes 786436
Sparse Core Ops, SparseCore 0:
  10.1 77.7 all-gather.2
  124.2 46.5 all-gather.4
  324.5 59.0 reduce-scatter.3
where the time goes:
time: 392 us
  waiting for transfers between devices  324 us (83%)
  other arithmetic  23.9 us (6%)
  matrix products  16.7 us (4%)
  between operations  13.9 us (4%)
  local copies, waits for them, and re-layouts  10.9 us (3%)
    ppermute x2, waiting for transfers between devices, partner(): return lax.ppermute(block, axis, route)  142 us
    all_gather x1, waiting for transfers between devices, shards(): lax.all_gather(upper_factor, 'tile', axis=2, tiled=True)  79.8 us
    reduce_scatter x1, waiting for transfers between devices, shards(): lax.psum_scatter(partial_value, 'tile', scatter_dimension=0, tiled=True)  56 us
    all_gather x1, waiting for transfers between devices, shards(): segment = lax.all_gather(modes, 'tile', axis=0, tiled=True)  46.2 us
    add x2, other arithmetic, shards(): schur_part = schur_part + partner(schur_part, 'subtree', level_bit)  22.3 us
  transfers between devices with their start and end apart: 5, of which 5 were waited for; matrix products, arithmetic and copies ran while one was open for 2% of the time, Pallas kernels for 0%

commit v1 on v0

--- a/solution.py
+++ b/solution.py
@@ -5,6 +5,16 @@
 
 SPEED_STEPS = 64
 OMEGA_TOP = 2.0
+
+
+def turned_line(array, mesh_axis, along):
+    size = lax.axis_size(mesh_axis)
+    current, parts = (array, [array])
+    for _ in range(size - 1):
+        current = lax.ppermute(current, mesh_axis, [(i, (i + 1) % size) for i in range(size)])
+        parts.insert(0, current)
+    row_of_blocks = jnp.concatenate(parts, axis=along)
+    return jnp.roll(row_of_blocks, (lax.axis_index(mesh_axis) + 1) * array.shape[along], axis=along)
 
 
 def partner(block, axis, distance):
@@ -49,7 +59,7 @@
         schur_part = schur_part + partner(schur_part, "subtree", level_bit)
     schur_out = lax.dynamic_slice_in_dim(schur_part, own_first, own_width, 1)
     col_first = branch_pos * mode_cols
-    segment = lax.all_gather(modes, "tile", axis=0, tiled=True)
+    segment = turned_line(modes, "tile", 0)
     row_count = segment.shape[0]
     wanted = lax.dynamic_slice_in_dim(segment, col_first, mode_cols, 1).astype(jnp.float32)
     response = jnp.dot(

time: 392 us -> 393 us (level)
  waiting for transfers between devices: 324 us -> 319 us
    ppermute x0 -> x7, waiting for transfers between devices: none -> 64.3 us  [turned_line(): lax.ppermute(current, mesh_axis, [(i, (i + 1) % size) for i in range(size)])]
    all_gather x1 -> x0, waiting for transfers between devices: 46.2 us -> none  [shards(): segment = lax.all_gather(modes, 'tile', axis=0, tiled=True)]
    ppermute x2, waiting for transfers between devices: 142 us -> 119 us  [partner(): return lax.ppermute(block, axis, route)]
  transfers between devices with their start and end apart: 5 -> 11, of which waited for: 5 -> 11; matrix products, arithmetic and copies ran while one was open for 2% -> 3% of each run, Pallas kernels for 0% -> 0%
where the time goes in v1:
time: 393 us
  waiting for transfers between devices  319 us (81%)
  other arithmetic  24 us (6%)
  matrix products  19.6 us (5%)
  between operations  14.3 us (4%)
  local copies, waits for them, and re-layouts  12.8 us (3%)
    ppermute x2, waiting for transfers between devices, partner(): return lax.ppermute(block, axis, route)  119 us
    all_gather x1, waiting for transfers between devices, shards(): lax.all_gather(upper_factor, 'tile', axis=2, tiled=True)  79.8 us
    ppermute x7, waiting for transfers between devices, turned_line(): lax.ppermute(current, mesh_axis, [(i, (i + 1) % size) for i in range(size)])  64.3 us
    reduce_scatter x1, waiting for transfers between devices, shards(): lax.psum_scatter(partial_value, 'tile', scatter_dimension=0, tiled=True)  55.7 us
    add x2, other arithmetic, shards(): schur_part = schur_part + partner(schur_part, 'subtree', level_bit)  22.3 us
    dot_general x1, matrix products, shards(): jnp.dot(schur_part, wanted, precision=lax.Precision.HIGHEST, preferred_el...  8.09 us
  transfers between devices with their start and end apart: 11, of which 11 were waited for; matrix products, arithmetic and copies ran while one was open for 3% of the time, Pallas kernels for 0%

profile of v1, /device:TPU:0, one launch (start us, length us, event | category | flops | bytes accessed | tf_op | source)
XLA Modules:
  0.0 392.9 jit_solution(16566173384467039758)
XLA Ops:
  8.0 79.8 %all-gather.2.cloned.1.call-done = bf16[1,512,4096]{2,1,0:T(8,128)(2,1)} async-done(((bf16[1,512,512]{2,1,0:T(8,128)(2,1)}), bf16[1,512,4096]{2,1,0:T(8,128)(2,1)}) %all-gather.2.cloned.1.call-update) | async-done | bytes 4194320 | tf_op jit(solution)/shard_map/all_gather | solution.py:50
  87.8 7.0 %bitcast_subtract_fusion = f32[512,4096]{1,0:T(8,128)S(1)} fusion(f32[1,512,4096]{2,1,0:T(8,128)} %param.8, bf16[1,512,4096]{2,1,0:T(8,128)(2,1)} %all-gather.2.cloned.1.call-done, bf16[1,512,512]{2,1,0:T(8,128)(2,1)S(1)} %copy-done), kind=kOutput, calls=%fused_computation.1 | convolution fusion | flops 2149580800 | bytes 21495808 | tf_op jit(solution)/shard_map/lrk,lkn->rn/dot_general | solution.py:47
  94.8 3.2 copy-done.2
  98.1 13.3 %collective-permute-done = f32[512,4096]{1,0:T(8,128)} collective-permute-done((f32[512,4096]{1,0:T(8,128)S(1)}, f32[512,4096]{1,0:T(8,128)}, u32[]{:S(2)}, u32[]{:S(2)}) %collective-permute-start) | collective-permute-done | bytes 8388640 | tf_op jit(solution)/shard_map/ppermute | solution.py:27
  111.4 11.2 %add.50 = f32[512,4096]{1,0:T(8,128)} add(f32[512,4096]{1,0:T(8,128)} %copy-done.2, f32[512,4096]{1,0:T(8,128)} %collective-permute-done) | non-fusion elementwise | flops 2097152 | bytes 25165824 | tf_op jit(solution)/shard_map/add | solution.py:59
  122.6 1.5 collective-permute-start.1
  124.1 1.4 collective-permute-start.2
  125.5 9.3 %collective-permute-done.2 = bf16[512,256]{1,0:T(8,128)(2,1)S(1)} collective-permute-done((bf16[512,256]{1,0:T(8,128)(2,1)S(1)}, bf16[512,256]{1,0:T(8,128)(2,1)S(1)}, u32[]{:S(2)}, u32[]{:S(2)}) %collective-permute-start.2) | collective-permute-done | bytes 262176 | tf_op jit(solution)/shard_map/ppermute | solution.py:14
  134.8 9.9 %collective-permute-done.3 = bf16[512,256]{1,0:T(8,128)(2,1)S(1)} collective-permute-done((bf16[512,256]{1,0:T(8,128)(2,1)S(1)}, bf16[512,256]{1,0:T(8,128)(2,1)S(1)}, u32[]{:S(2)}, u32[]{:S(2)}) %collective-permute-start.3) | collective-permute-done | bytes 262176 | tf_op jit(solution)/shard_map/ppermute | solution.py:14
  144.7 9.1 %collective-permute-done.4 = bf16[512,256]{1,0:T(8,128)(2,1)S(1)} collective-permute-done((bf16[512,256]{1,0:T(8,128)(2,1)S(1)}, bf16[512,256]{1,0:T(8,128)(2,1)S(1)}, u32[]{:S(2)}, u32[]{:S(2)}) %collective-permute-start.4) | collective-permute-done | bytes 262176 | tf_op jit(solution)/shard_map/ppermute | solution.py:14
  153.8 9.1 %collective-permute-done.5 = bf16[512,256]{1,0:T(8,128)(2,1)S(1)} collective-permute-done((bf16[512,256]{1,0:T(8,128)(2,1)S(1)}, bf16[512,256]{1,0:T(8,128)(2,1)S(1)}, u32[]{:S(2)}, u32[]{:S(2)}) %collective-permute-start.5) | collective-permute-done | bytes 262176 | tf_op jit(solution)/shard_map/ppermute | solution.py:14
  162.9 9.1 %collective-permute-done.6 = bf16[512,256]{1,0:T(8,128)(2,1)S(1)} collective-permute-done((bf16[512,256]{1,0:T(8,128)(2,1)S(1)}, bf16[512,256]{1,0:T(8,128)(2,1)S(1)}, u32[]{:S(2)}, u32[]{:S(2)}) %collective-permute-start.6) | collective-permute-done | bytes 262176 | tf_op jit(solution)/shard_map/ppermute | solution.py:14
  172.0 10.1 %collective-permute-done.7 = bf16[512,256]{1,0:T(8,128)(2,1)S(1)} collective-permute-done((bf16[512,256]{1,0:T(8,128)(2,1)S(1)}, bf16[512,256]{1,0:T(8,128)(2,1)S(1)}, u32[]{:S(2)}, u32[]{:S(2)}) %collective-permute-start.7) | collective-permute-done | bytes 262176 | tf_op jit(solution)/shard_map/ppermute | solution.py:14
  182.2 1.3 copy.13
  183.5 7.7 %collective-permute-done.8 = bf16[512,256]{1,0:T(8,128)(2,1)S(1)} collective-permute-done((bf16[512,256]{1,0:T(8,128)(2,1)S(1)}, bf16[512,256]{1,0:T(8,128)(2,1)S(1)}, u32[]{:S(2)}, u32[]{:S(2)}) %collective-permute-start.8) | collective-permute-done | bytes 262176 | tf_op jit(solution)/shard_map/ppermute | solution.py:14
  191.7 1.9 copy-done.4
  193.7 2.0 gather_fusion
  196.7 2.6 fusion.2
  200.0 105.3 %collective-permute-done.1 = f32[512,4096]{1,0:T(8,128)} collective-permute-done((f32[512,4096]{1,0:T(8,128)}, f32[512,4096]{1,0:T(8,128)}, u32[]{:S(2)}, u32[]{:S(2)}) %collective-permute-start.1) | collective-permute-done | bytes 8388640 | tf_op jit(solution)/shard_map/ppermute | solution.py:27
  305.4 11.2 %add.51 = f32[512,4096]{1,0:T(8,128)} add(f32[512,4096]{1,0:T(8,128)} %add.50, f32[512,4096]{1,0:T(8,128)} %collective-permute-done.1) | non-fusion elementwise | flops 2097152 | bytes 25165824 | tf_op jit(solution)/shard_map/add | solution.py:59
  316.6 8.1 %fusion.4 = f32[512,64]{1,0:T(8,128)S(1)} fusion(f32[512,4096]{1,0:T(8,128)} %add.51, bf16[8192,256]{1,0:T(8,128)(2,1)} %copy-done.4, s32[]{:T(128)S(6)} %select_n.43, s32[]{:T(128)S(6)} %select_n.45), kind=kOutput, calls=%fused_computation.7 | convolution fusion | flops 1610612736 | bytes 9568264 | tf_op jit(solution)/shard_map/dot_general | solution.py:65
  325.8 3.2 constant_dynamic-slice_fusion.1
  329.0 55.7 %reduce-scatter.4.cloned.1.call-done = f32[32,64]{1,0:T(8,128)} async-done(((f32[256,64]{1,0:T(8,128)}), f32[32,64]{1,0:T(8,128)}) %reduce-scatter.4.cloned.1.call-update) | async-done | bytes 8208 | tf_op jit(solution)/shard_map/reduce_scatter | solution.py:80
  384.6 1.4 multiply_subtract_fusion
  (53 shorter events, 4.2 us)
Async XLA Ops:
  7.2 80.6 %copy-start = (bf16[1,512,512]{2,1,0:T(8,128)(2,1)S(1)}, bf16[1,512,512]{2,1,0:T(8,128)(2,1)}, u32[]{:S(2)}) copy-start(bf16[1,512,512]{2,1,0:T(8,128)(2,1)} %param.9) | copy-start | bytes 1572868
  7.2 80.6 %all-gather.2.cloned.1.call-start = ((), (), s32[]{:S(2)}) async-start(), calls=%async_computation.1 | async-start | bytes 4718592 | tf_op jit(solution)/shard_map/all_gather | solution.py:50
  7.9 376.7 %reduce-scatter.4.cloned.1.call-start = ((), (), s32[]{:S(2)}) async-start(), calls=%async_computation.2 | async-start | bytes 147456 | tf_op jit(solution)/shard_map/reduce_scatter | solution.py:80
  94.8 3.2 copy-start.2
  98.0 26.0 %copy-start.5 = (bf16[512,256]{1,0:T(8,128)(2,1)S(1)}, bf16[512,256]{1,0:T(8,128)(2,1)}, u32[]{:S(2)}) copy-start(bf16[512,256]{1,0:T(8,128)(2,1)} %param.11) | copy-start | bytes 786436
  98.0 73.9 %copy-start.8 = (s32[2]{0:T(128)S(1)}, s32[2]{0:T(128)}, u32[]{:S(2)}) copy-start(s32[2]{0:T(128)} %param.15) | copy-start | bytes 28
  98.0 73.9 %copy-start.6 = (s32[512]{0:T(512)S(1)}, s32[512]{0:T(512)}, u32[]{:S(2)}) copy-start(s32[512]{0:T(512)} %param.12) | copy-start | bytes 6148
  98.1 84.1 %copy-start.3 = (f32[512,512]{1,0:T(8,128)S(1)}, f32[512,512]{1,0:T(8,128)}, u32[]{:S(2)}) copy-start(f32[512,512]{1,0:T(8,128)} %param.13) | copy-start | bytes 3145732
  98.1 13.4 %collective-permute-start = (f32[512,4096]{1,0:T(8,128)S(1)}, f32[512,4096]{1,0:T(8,128)}, u32[]{:S(2)}, u32[]{:S(2)}) collective-permute-start(f32[512,4096]{1,0:T(8,128)S(1)} %bitcast_subtract_fusion), channel_id=1, source_target_pairs={{0,8},{8,0},{16,24},{24,16},{1,9},{9,1},{17,25},{25,17},{2,10},{10... | collective-permute-start | bytes 25165832 | tf_op jit(solution)/shard_map/ppermute | solution.py:27
  122.6 182.8 %collective-permute-start.1 = (f32[512,4096]{1,0:T(8,128)}, f32[512,4096]{1,0:T(8,128)}, u32[]{:S(2)}, u32[]{:S(2)}) collective-permute-start(f32[512,4096]{1,0:T(8,128)} %add.50), channel_id=1, source_target_pairs={{0,16},{16,0},{8,24},{24,8},{1,17},{17,1},{9,25},{25,9},{2,18},{18... | collective-permute-start | bytes 25165832 | tf_op jit(solution)/shard_map/ppermute | solution.py:27
  124.1 10.8 %collective-permute-start.2 = (bf16[512,256]{1,0:T(8,128)(2,1)S(1)}, bf16[512,256]{1,0:T(8,128)(2,1)S(1)}, u32[]{:S(2)}, u32[]{:S(2)}) collective-permute-start(bf16[512,256]{1,0:T(8,128)(2,1)S(1)} %copy-done.5), channel_id=1, source_target_pairs={{0,1},{1,2},{2,3},{3,4},{4,5},{5,6},{6,7},{7,0},{8,9},{9,10},{10,1... | collective-permute-start | bytes 786440 | tf_op jit(solution)/shard_map/ppermute | solution.py:14
  134.8 9.9 %collective-permute-start.3 = (bf16[512,256]{1,0:T(8,128)(2,1)S(1)}, bf16[512,256]{1,0:T(8,128)(2,1)S(1)}, u32[]{:S(2)}, u32[]{:S(2)}) collective-permute-start(bf16[512,256]{1,0:T(8,128)(2,1)S(1)} %collective-permute-done.2), channel_id=1, source_target_pairs={{0,1},{1,2},{2,3},{3,4},{4,5},{5,6},{6,7},{7,0},{8,9},{9,10},{10,1... | collective-permute-start | bytes 786440 | tf_op jit(solution)/shard_map/ppermute | solution.py:14
  144.7 9.1 %collective-permute-start.4 = (bf16[512,256]{1,0:T(8,128)(2,1)S(1)}, bf16[512,256]{1,0:T(8,128)(2,1)S(1)}, u32[]{:S(2)}, u32[]{:S(2)}) collective-permute-start(bf16[512,256]{1,0:T(8,128)(2,1)S(1)} %collective-permute-done.3), channel_id=1, source_target_pairs={{0,1},{1,2},{2,3},{3,4},{4,5},{5,6},{6,7},{7,0},{8,9},{9,10},{10,1... | collective-permute-start | bytes 786440 | tf_op jit(solution)/shard_map/ppermute | solution.py:14
  153.8 9.1 %collective-permute-start.5 = (bf16[512,256]{1,0:T(8,128)(2,1)S(1)}, bf16[512,256]{1,0:T(8,128)(2,1)S(1)}, u32[]{:S(2)}, u32[]{:S(2)}) collective-permute-start(bf16[512,256]{1,0:T(8,128)(2,1)S(1)} %collective-permute-done.4), channel_id=1, source_target_pairs={{0,1},{1,2},{2,3},{3,4},{4,5},{5,6},{6,7},{7,0},{8,9},{9,10},{10,1... | collective-permute-start | bytes 786440 | tf_op jit(solution)/shard_map/ppermute | solution.py:14
  162.9 9.1 %collective-permute-start.6 = (bf16[512,256]{1,0:T(8,128)(2,1)S(1)}, bf16[512,256]{1,0:T(8,128)(2,1)S(1)}, u32[]{:S(2)}, u32[]{:S(2)}) collective-permute-start(bf16[512,256]{1,0:T(8,128)(2,1)S(1)} %collective-permute-done.5), channel_id=1, source_target_pairs={{0,1},{1,2},{2,3},{3,4},{4,5},{5,6},{6,7},{7,0},{8,9},{9,10},{10,1... | collective-permute-start | bytes 786440 | tf_op jit(solution)/shard_map/ppermute | solution.py:14
  172.0 10.2 %collective-permute-start.7 = (bf16[512,256]{1,0:T(8,128)(2,1)S(1)}, bf16[512,256]{1,0:T(8,128)(2,1)S(1)}, u32[]{:S(2)}, u32[]{:S(2)}) collective-permute-start(bf16[512,256]{1,0:T(8,128)(2,1)S(1)} %collective-permute-done.6), channel_id=1, source_target_pairs={{0,1},{1,2},{2,3},{3,4},{4,5},{5,6},{6,7},{7,0},{8,9},{9,10},{10,1... | collective-permute-start | bytes 786440 | tf_op jit(solution)/shard_map/ppermute | solution.py:14
  182.1 9.1 %collective-permute-start.8 = (bf16[512,256]{1,0:T(8,128)(2,1)S(1)}, bf16[512,256]{1,0:T(8,128)(2,1)S(1)}, u32[]{:S(2)}, u32[]{:S(2)}) collective-permute-start(bf16[512,256]{1,0:T(8,128)(2,1)S(1)} %collective-permute-done.7), channel_id=1, source_target_pairs={{0,1},{1,2},{2,3},{3,4},{4,5},{5,6},{6,7},{7,0},{8,9},{9,10},{10,1... | collective-permute-start | bytes 786440 | tf_op jit(solution)/shard_map/ppermute | solution.py:14
  191.6 4.3 %copy-start.7 = (f32[512]{0:T(512)S(1)}, f32[512]{0:T(512)}, u32[]{:S(2)}) copy-start(f32[512]{0:T(512)} %param.14) | copy-start | bytes 6148
  191.6 1.9 copy-start.4
  316.6 69.5 %copy-start.1 = (bf16[1,512,512]{2,1,0:T(8,128)(2,1)S(1)}, bf16[1,512,512]{2,1,0:T(8,128)(2,1)}, u32[]{:S(2)}) copy-start(bf16[1,512,512]{2,1,0:T(8,128)(2,1)} %param.9) | copy-start | bytes 1572868
Sparse Core Ops, SparseCore 0:
  10.1 77.7 all-gather.1
  325.9 58.6 reduce-scatter.3
